TPU v7x, 256 devices: a whole 4x4x8 slice. The times are simulated.
256 devices in a mesh: seq: 64 (over x, z, core), ch: 4 (over y).
Axes of the slice: x: 4, y: 4, z: 8, core: 2. Of those that a mesh axis runs over, the one named last changes fastest.
Arguments:
- proj: bfloat16 [3, 128, 65536], P(None, 'ch', 'seq'), may hold values from -6 to 6
- cotangent: bfloat16 [128, 65536], P('ch', 'seq'), may hold values from -6 to 6
- short_w: float32 [3, 128, 3], P(None, 'ch'), may hold values from -3.5 to 3.5
- filter_in: float32 [32, 64], replicated, may hold values from -5 to 5
- filter_out: float32 [64, 128], P(None, 'ch'), may hold values from -0.75 to 0.75
- rates: float32 [128], P('ch'), may hold values from 0.25 to 2184
Outputs:
- grad_proj: bfloat16 [3, 128, 65536], P(None, 'ch', 'seq')
- grad_short: float32 [3, 128, 3], P(None, 'ch')
- grad_filter_out: float32 [64, 128], P(None, 'ch')
- grad_filter_in: float32 [32, 64], replicated
All inputs are finite; a program needn't handle non-finite values.
Results may differ from a plain program's by a relative error of at most 0.0013.
Values may be sent and summed in bfloat16 or wider, within the bound.
A program may use at most 64 MiB of HBM per device.

v0:
```python
import math
import jax
import jax.numpy as jnp
from jax import lax
from jax.sharding import PartitionSpec as P

PRECISE = lax.Precision.HIGHEST


def shifted(value, axis, by):
    length = lax.axis_size(axis)
    pairs = [(i, i + by) for i in range(length) if 0 <= i + by < length]
    return lax.ppermute(value, axis, pairs)


def position_features(positions, length, feature_count):
    feature_index = jnp.arange(feature_count, dtype=jnp.int32)
    multiplier = (1 + feature_index // 2 * 499) % length
    upper = positions // 1024
    lower = positions % 1024
    phases = (
        upper[:, None] * (multiplier * 1024 % length)[None, :]
        + lower[:, None] * multiplier[None, :]
    ) % length
    angles = phases.astype(jnp.float32) * (2.0 * math.pi / length)
    return jnp.where((feature_index % 2 == 0)[None, :], jnp.cos(angles), jnp.sin(angles))


def angle_tables(row_count, col_count, row_start, col_start, modulus):
    row_index = row_start + jnp.arange(row_count, dtype=jnp.int32)
    col_index = col_start + jnp.arange(col_count, dtype=jnp.int32)
    phases = row_index[:, None] * col_index[None, :] % modulus
    angles = phases.astype(jnp.float32) * (2.0 * math.pi / modulus)
    return (jnp.cos(angles), jnp.sin(angles))


def rotate(real_part, imag_part, cosine, sine, sign):
    return (
        real_part * cosine - sign * imag_part * sine,
        imag_part * cosine + sign * real_part * sine,
    )


def dft_axis(real_part, imag_part, form, cosine, sine, sign):
    real_cos = jnp.einsum(form, real_part, cosine, precision=PRECISE)
    real_sin = jnp.einsum(form, real_part, sine, precision=PRECISE)
    imag_cos = jnp.einsum(form, imag_part, cosine, precision=PRECISE)
    imag_sin = jnp.einsum(form, imag_part, sine, precision=PRECISE)
    return (real_cos - sign * imag_sin, imag_cos + sign * real_sin)


def shards(proj, cotangent, short_w, filter_in, filter_out, rates):
    tap_count = short_w.shape[2]
    channels = proj.shape[1]
    devices = lax.axis_size("seq")
    tokens_here = proj.shape[2]
    length = devices * tokens_here
    modulus = 2 * length
    norm_scale = 1.0 / math.sqrt(length)
    column_width = tokens_here // devices
    first_split = math.gcd(tokens_here, 64)
    second_split = tokens_here // first_split
    device_index = lax.axis_index("seq")
    rim_cols = shifted(proj[:, :, tokens_here - (tap_count - 1) :], "seq", 1)
    extended = jnp.concatenate([rim_cols, proj], 2).astype(jnp.float32)

    def delayed(offset):
        return extended[:, :, tap_count - 1 - offset : tap_count - 1 - offset + tokens_here]

    mixed_all = short_w[:, :, 0, None] * delayed(0)
    for offset in range(1, tap_count):
        mixed_all = mixed_all + short_w[:, :, offset, None] * delayed(offset)
    query_part, key_part, value_part = (mixed_all[0], mixed_all[1], mixed_all[2])
    gated_prod = key_part * value_part
    cotangent_full = cotangent.astype(jnp.float32)
    grad_conv = cotangent_full * query_part
    both_signals = jnp.concatenate([gated_prod, grad_conv], 0).reshape(2 * channels, 1, tokens_here)
    columns = lax.all_to_all(both_signals, "seq", split_axis=2, concat_axis=1, tiled=True)
    block_start = jnp.arange(devices, dtype=jnp.int32) * tokens_here
    offset_start = device_index * column_width + jnp.arange(column_width, dtype=jnp.int32)
    column_pos = (block_start[:, None] + offset_start[None, :]).reshape(devices * column_width)
    features = position_features(column_pos, length, filter_in.shape[0])
    preact = jnp.dot(features, filter_in, precision=PRECISE, preferred_element_type=jnp.float32)
    hidden = jnp.sin(preact)
    modulated = jnp.einsum("to,oc->ct", hidden, filter_out, precision=PRECISE)
    relative = column_pos.astype(jnp.float32) / length
    spread = jnp.sqrt(jnp.expm1(-2.0 * rates) / jnp.expm1(-2.0 * rates / length))
    envelope = jnp.exp(-rates[:, None] * relative[None, :]) / spread[:, None]
    kernel = (envelope * modulated).reshape(channels, devices, column_width)
    stacked = jnp.concatenate([columns[:channels], kernel, columns[channels:]], 0)
    cos_outer, sin_outer = angle_tables(devices, 2 * devices, 0, 0, 2 * devices)
    turned_real = jnp.einsum("ran,ak->rkn", stacked, cos_outer, precision=PRECISE)
    turned_imag = -jnp.einsum("ran,ak->rkn", stacked, sin_outer, precision=PRECISE)
    cos_turn, sin_turn = angle_tables(
        2 * devices, column_width, 0, device_index * column_width, modulus
    )
    turned_real, turned_imag = rotate(turned_real, turned_imag, cos_turn, sin_turn, -1.0)
    moved_real, moved_imag = (
        lax.all_to_all(turned_real, "seq", split_axis=1, concat_axis=2, tiled=True),
        lax.all_to_all(turned_imag, "seq", split_axis=1, concat_axis=2, tiled=True),
    )
    row_total = moved_real.shape[0]
    cos_first, sin_first = angle_tables(first_split, first_split, 0, 0, first_split)
    cos_second, sin_second = angle_tables(second_split, second_split, 0, 0, second_split)
    cos_mid, sin_mid = angle_tables(first_split, second_split, 0, 0, tokens_here)
    grid_real = moved_real.reshape(row_total, 2, first_split, second_split)
    grid_imag = moved_imag.reshape(row_total, 2, first_split, second_split)
    grid_real, grid_imag = dft_axis(
        grid_real, grid_imag, "rkab,ac->rkcb", cos_first, sin_first, -1.0
    )
    grid_real, grid_imag = rotate(grid_real, grid_imag, cos_mid, sin_mid, -1.0)
    spec_real, spec_imag = dft_axis(
        grid_real, grid_imag, "rkcb,bd->rkcd", cos_second, sin_second, -1.0
    )
    gated_real, gated_imag = (spec_real[:channels], spec_imag[:channels])
    kernel_real, kernel_imag = (
        spec_real[channels : 2 * channels],
        spec_imag[channels : 2 * channels],
    )
    grad_real, grad_imag = (spec_real[2 * channels :], spec_imag[2 * channels :])
    conv_real = gated_real * kernel_real - gated_imag * kernel_imag
    conv_imag = gated_real * kernel_imag + gated_imag * kernel_real
    back_real = grad_real * kernel_real + grad_imag * kernel_imag
    back_imag = grad_imag * kernel_real - grad_real * kernel_imag
    kgrad_real = grad_real * gated_real + grad_imag * gated_imag
    kgrad_imag = grad_imag * gated_real - grad_real * gated_imag
    cos_back, sin_back = angle_tables(2, tokens_here, 2 * device_index, 0, modulus)
    cos_last, sin_last = angle_tables(2 * devices, devices, 0, 0, 2 * devices)
    real_part = jnp.concatenate([conv_real, back_real, kgrad_real], 0)
    rows = real_part.shape[0]
    part_real, part_imag = dft_axis(
        real_part,
        jnp.concatenate([conv_imag, back_imag, kgrad_imag], 0),
        "rkcd,db->rkcb",
        cos_second,
        sin_second,
        1.0,
    )
    part_real, part_imag = rotate(part_real, part_imag, cos_mid, sin_mid, 1.0)
    part_real, part_imag = dft_axis(
        part_real, part_imag, "rkcb,ca->rkab", cos_first, sin_first, 1.0
    )
    part_real = part_real.reshape(rows, 2, tokens_here)
    part_imag = part_imag.reshape(rows, 2, tokens_here)
    part_real, part_imag = rotate(part_real, part_imag, cos_back[None], sin_back[None], 1.0)
    spread_real = lax.all_to_all(part_real, "seq", split_axis=2, concat_axis=1, tiled=True)
    spread_imag = lax.all_to_all(part_imag, "seq", split_axis=2, concat_axis=1, tiled=True)
    real_out = jnp.einsum("rkn,ka->ran", spread_real, cos_last, precision=PRECISE)
    real_out = (real_out - jnp.einsum("rkn,ka->ran", spread_imag, sin_last, precision=PRECISE)) * (
        1.0 / modulus
    )
    conv_cols = real_out[:channels]
    gated_cols = real_out[channels : 2 * channels]
    kernel_grad = real_out[2 * channels :]
    returned = lax.all_to_all(
        jnp.concatenate([conv_cols, gated_cols], 0), "seq", split_axis=1, concat_axis=2, tiled=True
    )
    returned = returned.reshape(2 * channels, tokens_here)
    conv_out = returned[:channels]
    grad_gated = returned[channels:]
    grad_mixed = jnp.stack(
        [cotangent_full * conv_out, grad_gated * value_part, grad_gated * key_part]
    )
    short_part = jnp.stack(
        [jnp.sum(grad_mixed * delayed(offset), axis=2) for offset in range(tap_count)], axis=2
    )
    weighted = envelope * kernel_grad.reshape(channels, devices * column_width)
    out_part = jnp.einsum("to,ct->oc", hidden, weighted, precision=PRECISE)
    grad_hidden = jnp.einsum("ct,oc->to", weighted, filter_out, precision=PRECISE)
    in_part = jnp.einsum("tf,to->fo", features, grad_hidden * jnp.cos(preact), precision=PRECISE)
    next_rim = shifted(grad_mixed[:, :, : tap_count - 1], "seq", -1)
    grad_extended = jnp.concatenate([grad_mixed, next_rim], 2)
    result = short_w[:, :, 0, None] * grad_extended[:, :, 0:tokens_here]
    for offset in range(1, tap_count):
        result = (
            result
            + short_w[:, :, offset, None] * grad_extended[:, :, offset : offset + tokens_here]
        )
    grad_proj = result.astype(jnp.bfloat16)
    short_total, out_total = lax.psum((short_part, out_part), "seq")
    in_total = lax.psum(in_part, ("seq", "ch"))
    return (grad_proj, short_total * norm_scale, out_total * norm_scale, in_total * norm_scale)


def solution(mesh):
    placed = (
        P(None, "ch", "seq"),
        P("ch", "seq"),
        P(None, "ch", None),
        P(),
        P(None, "ch"),
        P("ch"),
    )
    return jax.shard_map(
        shards,
        mesh=mesh,
        in_specs=placed,
        out_specs=(P(None, "ch", "seq"), P(None, "ch", None), P(None, "ch"), P()),
        check_vma=False,
    )
```

profile of v0, /device:TPU:8, one launch (start us, length us, event | category | flops | bytes accessed | tf_op | source)
XLA Modules:
  0.0 598.5 jit_solution(10087766709720511439)
XLA Ops:
  1.5 1.7 collective-permute-start
  4.3 5.1 fusion.244
  12.4 3.8 reduce
  16.2 2.1 reshape.320
  18.3 13.3 %all-to-all-start = ((f32[64,1,1024]{2,1,0:T(1,128)}), f32[64,1,1024]{2,1,0:T(1,128)}, u32[]{:S(2)}, u32[]{:S(2)}) async-start(f32[64,1,1024]{2,1,0:T(1,128)} %reshape.320), calls=%async_computation | async-start | bytes 524288 | tf_op jit(solution)/shard_map/all_to_all | solution.py:78
  31.6 1.9 fusion.11
  33.5 1.9 copy.146
  35.4 2.0 copy.148
  37.6 5.8 all-to-all-done
  43.4 2.9 reduce.1
  46.4 2.4 reshape.321
  48.8 2.3 fusion.241
  52.2 1.7 convolution_negate_fusion
  53.9 2.9 add_bitcast_fusion.1
  56.9 2.5 copy.152
  59.4 6.3 %all-to-all-start.2 = ((f32[96,128,16]{0,2,1:T(8,128)}), f32[96,128,16]{0,2,1:T(8,128)}, u32[]{:S(2)}, u32[]{:S(2)}) async-start(f32[96,128,16]{0,2,1:T(8,128)} %copy.152), calls=%async_computation.2 | async-start | bytes 2097152 | tf_op jit(solution)/shard_map/all_to_all | solution.py:100
  65.6 2.5 copy.150
  68.2 25.5 %all-to-all-done.2 = f32[96,128,16]{0,2,1:T(8,128)} async-done(((f32[96,128,16]{0,2,1:T(8,128)}), f32[96,128,16]{0,2,1:T(8,128)}, u32[]{:S(2)}, u32[]{:S(2)}) %all-to-all-start.2) | async-done | bytes 786464 | tf_op jit(solution)/shard_map/all_to_all | solution.py:100
  93.7 7.2 %all-to-all-start.1 = ((f32[96,128,16]{0,2,1:T(8,128)}), f32[96,128,16]{0,2,1:T(8,128)}, u32[]{:S(2)}, u32[]{:S(2)}) async-start(f32[96,128,16]{0,2,1:T(8,128)} %copy.150), calls=%async_computation.1 | async-start | bytes 2097152 | tf_op jit(solution)/shard_map/all_to_all | solution.py:99
  101.4 3.8 fusion.14
  105.3 23.3 %all-to-all-done.1 = f32[96,128,16]{0,2,1:T(8,128)} async-done(((f32[96,128,16]{0,2,1:T(8,128)}), f32[96,128,16]{0,2,1:T(8,128)}, u32[]{:S(2)}, u32[]{:S(2)}) %all-to-all-start.1) | async-done | bytes 786464 | tf_op jit(solution)/shard_map/all_to_all | solution.py:99
  128.5 2.9 fusion.18
  131.5 2.9 fusion.7
  134.4 3.4 subtract_bitcast_fusion
  137.8 1.6 fusion.29
  139.4 1.6 fusion.33
  141.0 1.7 fusion.5
  142.7 1.8 fusion.6
  151.2 1.9 multiply_subtract_fusion
  154.5 1.6 fusion.27
  160.1 1.7 fusion.13
  161.8 1.8 copy.166
  163.5 6.8 %all-to-all-start.3 = ((f32[96,2,1024]{0,1,2:T(2,128)}), f32[96,2,1024]{0,1,2:T(2,128)}, u32[]{:S(2)}, u32[]{:S(2)}) async-start(f32[96,2,1024]{0,1,2:T(2,128)} %copy.166), calls=%async_computation.3 | async-start | bytes 2097152 | tf_op jit(solution)/shard_map/all_to_all | solution.py:146
  170.4 3.0 copy.170
  173.4 25.0 %all-to-all-done.3 = f32[96,2,1024]{0,1,2:T(2,128)} async-done(((f32[96,2,1024]{0,1,2:T(2,128)}), f32[96,2,1024]{0,1,2:T(2,128)}, u32[]{:S(2)}, u32[]{:S(2)}) %all-to-all-start.3) | async-done | bytes 786464 | tf_op jit(solution)/shard_map/all_to_all | solution.py:146
  198.4 6.8 %all-to-all-start.4 = ((f32[96,2,1024]{0,1,2:T(2,128)}), f32[96,2,1024]{0,1,2:T(2,128)}, u32[]{:S(2)}, u32[]{:S(2)}) async-start(f32[96,2,1024]{0,1,2:T(2,128)} %copy.170), calls=%async_computation.4 | async-start | bytes 2097152 | tf_op jit(solution)/shard_map/all_to_all | solution.py:147
  206.7 1.8 fusion.21
  208.5 24.7 %all-to-all-done.4 = f32[96,2,1024]{0,1,2:T(2,128)} async-done(((f32[96,2,1024]{0,1,2:T(2,128)}), f32[96,2,1024]{0,1,2:T(2,128)}, u32[]{:S(2)}, u32[]{:S(2)}) %all-to-all-start.4) | async-done | bytes 786464 | tf_op jit(solution)/shard_map/all_to_all | solution.py:147
  238.8 2.1 reshape.322
  240.9 7.0 %all-to-all-start.5 = ((f32[64,1,1024]{2,1,0:T(1,128)}), f32[64,1,1024]{2,1,0:T(1,128)}, u32[]{:S(2)}, u32[]{:S(2)}) async-start(f32[64,1,1024]{2,1,0:T(1,128)} %reshape.322), calls=%async_computation.5 | async-start | bytes 524288 | tf_op jit(solution)/shard_map/all_to_all | solution.py:155
  247.8 2.2 copy.175
  250.0 1.9 copy.176
  251.9 2.2 convolution_multiply_fusion.4
  254.1 3.0 fusion.43
  257.1 75.9 %psum.23 = f32[32,64]{1,0:T(8,128)S(1)} all-reduce(f32[32,64]{1,0:T(8,128)S(1)} %fusion.43), channel_id=1, replica_groups=mesh['seq'=64,'ch'=4] {'seq','ch'}, use_global_device_ids=true, to_apply=%region_5.6 | all-reduce | flops 2048 | bytes 16384 | tf_op jit(solution)/shard_map/psum | solution.py:181
  334.4 2.9 reduce.2
  337.4 1.9 reshape.323
  346.4 250.5 %all-reduce = (f32[3,32,3]{1,0,2:T(4,128)S(1)}, f32[64,32]{0,1:T(8,128)S(1)}) all-reduce(f32[3,32,3]{1,0,2:T(4,128)S(1)} %pad_maximum_fusion.7, f32[64,32]{0,1:T(8,128)S(1)} %fusion.238), channel_id=1, replica_groups=mesh['seq'=64,'ch'=4] {'seq'}, use_global_device_ids=true, to_apply=%region_3.4 | all-reduce | flops 2336 | bytes 18688 | tf_op jit(solution)/shard_map/psum | solution.py:180
  (94 shorter events, 35.0 us)
Async XLA Ops:
  0.6 3.7 copy-start
  0.6 8.8 %copy-start.6 = (bf16[32,1024]{1,0:T(8,128)(2,1)S(1)}, bf16[32,1024]{1,0:T(8,128)(2,1)}, u32[]{:S(2)}) copy-start(bf16[32,1024]{1,0:T(8,128)(2,1)} %param.7) | copy-start | bytes 196612
  1.5 8.1 %collective-permute-start = (bf16[3,32,2]{2,1,0:T(8,128)(2,1)S(1)}, bf16[3,32,2]{2,1,0:T(8,128)(2,1)S(1)}, u32[]{:S(2)}, u32[]{:S(2)}) collective-permute-start(bf16[3,32,2]{2,1,0:T(8,128)(2,1)S(1)} %slice.96), channel_id=1, source_target_pairs={{0,4},{4,8},{8,12},{12,16},{16,20},{20,24},{24,28},{28,32},{32,36}... | collective-permute-start | bytes 1160 | tf_op jit(solution)/shard_map/ppermute | solution.py:13
  3.3 6.3 %copy-start.10 = (s32[32]{0:T(128)}, s32[32]{0:T(128)S(1)}, u32[]{:S(2)}) copy-start(s32[32]{0:T(128)S(1)} %get-tuple-element.66) | copy-start | bytes 388
  3.3 6.3 %copy-start.12 = (pred[32]{0:T(512)(128)(4,1)}, pred[32]{0:T(512)(128)(4,1)S(1)}, u32[]{:S(2)}) copy-start(pred[32]{0:T(512)(128)(4,1)S(1)} %fusion.143) | copy-start | bytes 100
  4.3 5.3 copy-start.5
  11.9 19.7 %copy-start.9 = (f32[32]{0:T(128)S(1)}, f32[32]{0:T(128)}, u32[]{:S(2)}) copy-start(f32[32]{0:T(128)} %param.11) | copy-start | bytes 388
  11.9 19.7 %copy-start.7 = (f32[64,32]{0,1:T(8,128)S(1)}, f32[64,32]{0,1:T(8,128)}, u32[]{:S(2)}) copy-start(f32[64,32]{0,1:T(8,128)} %param.10) | copy-start | bytes 24580
  18.3 25.2 %all-to-all-start = ((f32[64,1,1024]{2,1,0:T(1,128)}), f32[64,1,1024]{2,1,0:T(1,128)}, u32[]{:S(2)}, u32[]{:S(2)}) async-start(f32[64,1,1024]{2,1,0:T(1,128)} %reshape.320), calls=%async_computation | async-start | bytes 524288 | tf_op jit(solution)/shard_map/all_to_all | solution.py:78
  51.1 1.0 copy-start.2
  59.4 34.3 %all-to-all-start.2 = ((f32[96,128,16]{0,2,1:T(8,128)}), f32[96,128,16]{0,2,1:T(8,128)}, u32[]{:S(2)}, u32[]{:S(2)}) async-start(f32[96,128,16]{0,2,1:T(8,128)} %copy.152), calls=%async_computation.2 | async-start | bytes 2097152 | tf_op jit(solution)/shard_map/all_to_all | solution.py:100
  93.7 34.9 %all-to-all-start.1 = ((f32[96,128,16]{0,2,1:T(8,128)}), f32[96,128,16]{0,2,1:T(8,128)}, u32[]{:S(2)}, u32[]{:S(2)}) async-start(f32[96,128,16]{0,2,1:T(8,128)} %copy.150), calls=%async_computation.1 | async-start | bytes 2097152 | tf_op jit(solution)/shard_map/all_to_all | solution.py:99
  128.5 3.0 copy-start.3
  163.5 34.9 %all-to-all-start.3 = ((f32[96,2,1024]{0,1,2:T(2,128)}), f32[96,2,1024]{0,1,2:T(2,128)}, u32[]{:S(2)}, u32[]{:S(2)}) async-start(f32[96,2,1024]{0,1,2:T(2,128)} %copy.166), calls=%async_computation.3 | async-start | bytes 2097152 | tf_op jit(solution)/shard_map/all_to_all | solution.py:146
  198.4 34.9 %all-to-all-start.4 = ((f32[96,2,1024]{0,1,2:T(2,128)}), f32[96,2,1024]{0,1,2:T(2,128)}, u32[]{:S(2)}, u32[]{:S(2)}) async-start(f32[96,2,1024]{0,1,2:T(2,128)} %copy.170), calls=%async_computation.4 | async-start | bytes 2097152 | tf_op jit(solution)/shard_map/all_to_all | solution.py:147
  234.5 1.0 copy-start.4
  238.8 13.1 %copy-start.8 = (f32[64,32]{0,1:T(8,128)S(1)}, f32[64,32]{0,1:T(8,128)}, u32[]{:S(2)}) copy-start(f32[64,32]{0,1:T(8,128)} %param.10) | copy-start | bytes 24580
  240.9 13.2 %copy-start.11 = (s32[32]{0:T(128)S(1)}, s32[32]{0:T(128)}, u32[]{:S(2)}) copy-start(s32[32]{0:T(128)} %copy-done.10) | copy-start | bytes 388
  240.9 13.2 %copy-start.13 = (pred[32]{0:T(512)(128)(4,1)S(1)}, pred[32]{0:T(512)(128)(4,1)}, u32[]{:S(2)}) copy-start(pred[32]{0:T(512)(128)(4,1)} %copy-done.12) | copy-start | bytes 100
  240.9 93.6 %all-to-all-start.5 = ((f32[64,1,1024]{2,1,0:T(1,128)}), f32[64,1,1024]{2,1,0:T(1,128)}, u32[]{:S(2)}, u32[]{:S(2)}) async-start(f32[64,1,1024]{2,1,0:T(1,128)} %reshape.322), calls=%async_computation.5 | async-start | bytes 524288 | tf_op jit(solution)/shard_map/all_to_all | solution.py:155
  341.0 3.1 collective-permute-start.1
  344.1 253.9 %copy-start.1 = (f32[32,64]{1,0:T(8,128)S(1)}, f32[32,64]{1,0:T(8,128)}, u32[]{:S(2)}) copy-start(f32[32,64]{1,0:T(8,128)} %param.9) | copy-start | bytes 24580
where the time goes:
time: 605 us; the launch traced here: 599 us
  blocking collectives  326 us (54%)
  waiting for transfers between devices  106 us (18%)
  matrix products  52.9 us (9%)
  starting transfers between devices  50.4 us (8%)
  local copies, waits for them, and re-layouts  42.8 us (7%)
  other arithmetic  18.9 us (3%)
    psum x1, blocking collectives, shards(): short_total, out_total = lax.psum((short_part, out_part), 'seq')  250 us
    psum x1, blocking collectives, shards(): in_total = lax.psum(in_part, ('seq', 'ch'))  75.9 us
    all_to_all x1, waiting for transfers between devices, shards(): lax.all_to_all(turned_imag, 'seq', split_axis=1, concat_axis=2, tiled=True)  25.5 us
    all_to_all x1, waiting for transfers between devices, shards(): lax.all_to_all(part_real, 'seq', split_axis=2, concat_axis=1, tiled=True)  25 us
    all_to_all x1, waiting for transfers between devices, shards(): lax.all_to_all(part_imag, 'seq', split_axis=2, concat_axis=1, tiled=True)  24.7 us
    all_to_all x1, waiting for transfers between devices, shards(): lax.all_to_all(turned_real, 'seq', split_axis=1, concat_axis=2, tiled=True)  23.3 us
    all_to_all x1, starting transfers between devices, shards(): lax.all_to_all(both_signals, 'seq', split_axis=2, concat_axis=1, tiled=True)  13.3 us
    unnamed x38, local copies, waits for them, and re-layouts  12.3 us
  transfers between devices with their start and end apart: 8, of which 6 were waited for; matrix products, arithmetic and copies ran while one was open for 6% of the time, Pallas kernels for 0%

commit v1 on v0

--- a/solution.py
+++ b/solution.py
@@ -178,7 +178,9 @@
         )
     grad_proj = result.astype(jnp.bfloat16)
     short_total, out_total = lax.psum((short_part, out_part), "seq")
-    in_total = lax.psum(in_part, ("seq", "ch"))
+    in_total = in_part
+    for over in ("seq", "ch"):
+        in_total = lax.psum(in_total, over)
     return (grad_proj, short_total * norm_scale, out_total * norm_scale, in_total * norm_scale)
 
 

time: 605 us -> 546 us (0.902)
  blocking collectives: 326 us -> 264 us
    psum x1, blocking collectives: 75.9 us -> 14.1 us  [shards(): in_total = lax.psum(in_total, over)]
    unnamed x38 -> x42, local copies, waits for them, and re-layouts: 12.3 us -> 13.1 us
  transfers between devices with their start and end apart: 8 -> 8, of which waited for: 6 -> 6; matrix products, arithmetic and copies ran while one was open for 6% -> 7% of each run, Pallas kernels for 0% -> 0%
where the time goes in v1:
time: 546 us; the launch traced here: 538 us
  blocking collectives  264 us (48%)
  waiting for transfers between devices  108 us (20%)
  matrix products  53.6 us (10%)
  starting transfers between devices  50.3 us (9%)
  local copies, waits for them, and re-layouts  42.7 us (8%)
  other arithmetic  18.8 us (3%)
    psum x1, blocking collectives, shards(): short_total, out_total = lax.psum((short_part, out_part), 'seq')  249 us
    all_to_all x1, waiting for transfers between devices, shards(): lax.all_to_all(turned_imag, 'seq', split_axis=1, concat_axis=2, tiled=True)  25.5 us
    all_to_all x1, waiting for transfers between devices, shards(): lax.all_to_all(part_real, 'seq', split_axis=2, concat_axis=1, tiled=True)  25 us
    all_to_all x1, waiting for transfers between devices, shards(): lax.all_to_all(part_imag, 'seq', split_axis=2, concat_axis=1, tiled=True)  24.7 us
    all_to_all x1, waiting for transfers between devices, shards(): lax.all_to_all(turned_real, 'seq', split_axis=1, concat_axis=2, tiled=True)  23.3 us
    psum x1, blocking collectives, shards(): in_total = lax.psum(in_total, over)  14.1 us
    all_to_all x1, starting transfers between devices, shards(): lax.all_to_all(both_signals, 'seq', split_axis=2, concat_axis=1, tiled=True)  13.3 us
    unnamed x42, local copies, waits for them, and re-layouts  13.1 us
  transfers between devices with their start and end apart: 8, of which 6 were waited for; matrix products, arithmetic and copies ran while one was open for 7% of the time, Pallas kernels for 0%

profile of v1, /device:TPU:8, one launch (start us, length us, event | category | flops | bytes accessed | tf_op | source)
XLA Modules:
  0.0 538.4 jit_solution(1813360750721617488)
XLA Ops:
  1.5 1.7 collective-permute-start
  4.3 5.1 fusion.244
  12.4 3.8 reduce
  16.2 2.1 reshape.320
  18.3 13.3 %all-to-all-start = ((f32[64,1,1024]{2,1,0:T(1,128)}), f32[64,1,1024]{2,1,0:T(1,128)}, u32[]{:S(2)}, u32[]{:S(2)}) async-start(f32[64,1,1024]{2,1,0:T(1,128)} %reshape.320), calls=%async_computation | async-start | bytes 524288 | tf_op jit(solution)/shard_map/all_to_all | solution.py:78
  31.6 1.9 fusion.11
  33.5 1.9 copy.146
  35.4 2.0 copy.148
  37.6 5.9 %all-to-all-done = f32[64,1,1024]{2,1,0:T(1,128)} async-done(((f32[64,1,1024]{2,1,0:T(1,128)}), f32[64,1,1024]{2,1,0:T(1,128)}, u32[]{:S(2)}, u32[]{:S(2)}) %all-to-all-start) | async-done | bytes 262176 | tf_op jit(solution)/shard_map/all_to_all | solution.py:78
  43.4 2.9 reduce.1
  46.4 2.4 reshape.321
  48.8 2.3 fusion.241
  52.2 1.7 convolution_negate_fusion
  54.0 2.9 add_bitcast_fusion.1
  56.9 2.5 copy.152
  59.4 6.3 %all-to-all-start.2 = ((f32[96,128,16]{0,2,1:T(8,128)}), f32[96,128,16]{0,2,1:T(8,128)}, u32[]{:S(2)}, u32[]{:S(2)}) async-start(f32[96,128,16]{0,2,1:T(8,128)} %copy.152), calls=%async_computation.2 | async-start | bytes 2097152 | tf_op jit(solution)/shard_map/all_to_all | solution.py:100
  65.6 2.5 copy.150
  68.1 25.5 %all-to-all-done.2 = f32[96,128,16]{0,2,1:T(8,128)} async-done(((f32[96,128,16]{0,2,1:T(8,128)}), f32[96,128,16]{0,2,1:T(8,128)}, u32[]{:S(2)}, u32[]{:S(2)}) %all-to-all-start.2) | async-done | bytes 786464 | tf_op jit(solution)/shard_map/all_to_all | solution.py:100
  93.7 7.2 %all-to-all-start.1 = ((f32[96,128,16]{0,2,1:T(8,128)}), f32[96,128,16]{0,2,1:T(8,128)}, u32[]{:S(2)}, u32[]{:S(2)}) async-start(f32[96,128,16]{0,2,1:T(8,128)} %copy.150), calls=%async_computation.1 | async-start | bytes 2097152 | tf_op jit(solution)/shard_map/all_to_all | solution.py:99
  101.4 3.8 fusion.14
  105.3 23.3 %all-to-all-done.1 = f32[96,128,16]{0,2,1:T(8,128)} async-done(((f32[96,128,16]{0,2,1:T(8,128)}), f32[96,128,16]{0,2,1:T(8,128)}, u32[]{:S(2)}, u32[]{:S(2)}) %all-to-all-start.1) | async-done | bytes 786464 | tf_op jit(solution)/shard_map/all_to_all | solution.py:99
  128.5 2.9 fusion.18
  131.5 2.9 fusion.7
  134.4 3.4 subtract_bitcast_fusion
  137.8 1.6 fusion.29
  139.4 1.6 fusion.33
  141.1 1.7 fusion.5
  142.7 1.8 fusion.6
  151.2 1.9 multiply_subtract_fusion
  154.5 1.6 fusion.27
  160.1 1.6 fusion.13
  161.7 1.8 copy.166
  163.5 6.8 %all-to-all-start.3 = ((f32[96,2,1024]{0,1,2:T(2,128)}), f32[96,2,1024]{0,1,2:T(2,128)}, u32[]{:S(2)}, u32[]{:S(2)}) async-start(f32[96,2,1024]{0,1,2:T(2,128)} %copy.166), calls=%async_computation.3 | async-start | bytes 2097152 | tf_op jit(solution)/shard_map/all_to_all | solution.py:146
  170.3 3.1 copy.170
  173.4 25.0 %all-to-all-done.3 = f32[96,2,1024]{0,1,2:T(2,128)} async-done(((f32[96,2,1024]{0,1,2:T(2,128)}), f32[96,2,1024]{0,1,2:T(2,128)}, u32[]{:S(2)}, u32[]{:S(2)}) %all-to-all-start.3) | async-done | bytes 786464 | tf_op jit(solution)/shard_map/all_to_all | solution.py:146
  198.4 6.8 %all-to-all-start.4 = ((f32[96,2,1024]{0,1,2:T(2,128)}), f32[96,2,1024]{0,1,2:T(2,128)}, u32[]{:S(2)}, u32[]{:S(2)}) async-start(f32[96,2,1024]{0,1,2:T(2,128)} %copy.170), calls=%async_computation.4 | async-start | bytes 2097152 | tf_op jit(solution)/shard_map/all_to_all | solution.py:147
  206.6 1.9 fusion.21
  208.5 24.7 %all-to-all-done.4 = f32[96,2,1024]{0,1,2:T(2,128)} async-done(((f32[96,2,1024]{0,1,2:T(2,128)}), f32[96,2,1024]{0,1,2:T(2,128)}, u32[]{:S(2)}, u32[]{:S(2)}) %all-to-all-start.4) | async-done | bytes 786464 | tf_op jit(solution)/shard_map/all_to_all | solution.py:147
  238.5 2.1 reshape.322
  240.6 6.8 %all-to-all-start.5 = ((f32[64,1,1024]{2,1,0:T(1,128)}), f32[64,1,1024]{2,1,0:T(1,128)}, u32[]{:S(2)}, u32[]{:S(2)}) async-start(f32[64,1,1024]{2,1,0:T(1,128)} %reshape.322), calls=%async_computation.5 | async-start | bytes 524288 | tf_op jit(solution)/shard_map/all_to_all | solution.py:155
  249.8 1.9 copy.176
  253.1 2.9 convolution_multiply_fusion.4
  256.0 3.3 all-to-all-done.5
  259.3 2.9 reduce.2
  262.2 1.9 reshape.323
  267.1 3.0 fusion.43
  272.5 249.5 %all-reduce = (f32[3,32,3]{1,0,2:T(4,128)S(1)}, f32[64,32]{0,1:T(8,128)S(1)}, f32[32,64]{1,0:T(8,128)S(1)}) all-reduce(f32[3,32,3]{1,0,2:T(4,128)S(1)} %pad_maximum_fusion.7, f32[64,32]{0,1:T(8,128)S(1)} %fusion.238, f32[32,64]{1,0:T(8,128)S(1)} %fusion.43), channel_id=1, replica_groups=mesh['seq'=64,'ch'=4] {'seq'}, use_global_device_ids=true, to_apply=%region_3.4 | all-reduce | flops 4384 | bytes 35072 | tf_op jit(solution)/shard_map/psum | solution.py:180
  523.2 14.1 %psum.31 = f32[32,64]{1,0:T(8,128)S(1)} all-reduce(f32[32,64]{1,0:T(8,128)S(1)} %get-tuple-element.29), channel_id=1, replica_groups=mesh['seq'=64,'ch'=4] {'ch'}, use_global_device_ids=true, to_apply=%region_6.7 | all-reduce | flops 2048 | bytes 16384 | tf_op jit(solution)/shard_map/psum | solution.py:183
  (98 shorter events, 36.0 us)
Async XLA Ops:
  0.6 3.7 copy-start
  0.6 8.8 %copy-start.7 = (bf16[32,1024]{1,0:T(8,128)(2,1)S(1)}, bf16[32,1024]{1,0:T(8,128)(2,1)}, u32[]{:S(2)}) copy-start(bf16[32,1024]{1,0:T(8,128)(2,1)} %param.7) | copy-start | bytes 196612
  1.5 8.1 %collective-permute-start = (bf16[3,32,2]{2,1,0:T(8,128)(2,1)S(1)}, bf16[3,32,2]{2,1,0:T(8,128)(2,1)S(1)}, u32[]{:S(2)}, u32[]{:S(2)}) collective-permute-start(bf16[3,32,2]{2,1,0:T(8,128)(2,1)S(1)} %slice.96), channel_id=1, source_target_pairs={{0,4},{4,8},{8,12},{12,16},{16,20},{20,24},{24,28},{28,32},{32,36}... | collective-permute-start | bytes 1160 | tf_op jit(solution)/shard_map/ppermute | solution.py:13
  3.3 6.4 %copy-start.12 = (s32[32]{0:T(128)}, s32[32]{0:T(128)S(1)}, u32[]{:S(2)}) copy-start(s32[32]{0:T(128)S(1)} %get-tuple-element.67) | copy-start | bytes 388
  3.3 6.3 %copy-start.14 = (pred[32]{0:T(512)(128)(4,1)}, pred[32]{0:T(512)(128)(4,1)S(1)}, u32[]{:S(2)}) copy-start(pred[32]{0:T(512)(128)(4,1)S(1)} %fusion.143) | copy-start | bytes 100
  4.3 5.3 copy-start.6
  11.9 19.7 %copy-start.10 = (f32[32]{0:T(128)S(1)}, f32[32]{0:T(128)}, u32[]{:S(2)}) copy-start(f32[32]{0:T(128)} %param.11) | copy-start | bytes 388
  11.9 19.7 %copy-start.8 = (f32[64,32]{0,1:T(8,128)S(1)}, f32[64,32]{0,1:T(8,128)}, u32[]{:S(2)}) copy-start(f32[64,32]{0,1:T(8,128)} %param.10) | copy-start | bytes 24580
  18.3 25.2 %all-to-all-start = ((f32[64,1,1024]{2,1,0:T(1,128)}), f32[64,1,1024]{2,1,0:T(1,128)}, u32[]{:S(2)}, u32[]{:S(2)}) async-start(f32[64,1,1024]{2,1,0:T(1,128)} %reshape.320), calls=%async_computation | async-start | bytes 524288 | tf_op jit(solution)/shard_map/all_to_all | solution.py:78
  51.2 1.0 copy-start.2
  59.4 34.3 %all-to-all-start.2 = ((f32[96,128,16]{0,2,1:T(8,128)}), f32[96,128,16]{0,2,1:T(8,128)}, u32[]{:S(2)}, u32[]{:S(2)}) async-start(f32[96,128,16]{0,2,1:T(8,128)} %copy.152), calls=%async_computation.2 | async-start | bytes 2097152 | tf_op jit(solution)/shard_map/all_to_all | solution.py:100
  93.7 34.9 %all-to-all-start.1 = ((f32[96,128,16]{0,2,1:T(8,128)}), f32[96,128,16]{0,2,1:T(8,128)}, u32[]{:S(2)}, u32[]{:S(2)}) async-start(f32[96,128,16]{0,2,1:T(8,128)} %copy.150), calls=%async_computation.1 | async-start | bytes 2097152 | tf_op jit(solution)/shard_map/all_to_all | solution.py:99
  128.5 3.0 copy-start.4
  163.5 34.9 %all-to-all-start.3 = ((f32[96,2,1024]{0,1,2:T(2,128)}), f32[96,2,1024]{0,1,2:T(2,128)}, u32[]{:S(2)}, u32[]{:S(2)}) async-start(f32[96,2,1024]{0,1,2:T(2,128)} %copy.166), calls=%async_computation.3 | async-start | bytes 2097152 | tf_op jit(solution)/shard_map/all_to_all | solution.py:146
  198.4 34.9 %all-to-all-start.4 = ((f32[96,2,1024]{0,1,2:T(2,128)}), f32[96,2,1024]{0,1,2:T(2,128)}, u32[]{:S(2)}, u32[]{:S(2)}) async-start(f32[96,2,1024]{0,1,2:T(2,128)} %copy.170), calls=%async_computation.4 | async-start | bytes 2097152 | tf_op jit(solution)/shard_map/all_to_all | solution.py:147
  234.5 1.0 copy-start.5
  236.6 0.8 copy-start.3
  240.6 18.7 %all-to-all-start.5 = ((f32[64,1,1024]{2,1,0:T(1,128)}), f32[64,1,1024]{2,1,0:T(1,128)}, u32[]{:S(2)}, u32[]{:S(2)}) async-start(f32[64,1,1024]{2,1,0:T(1,128)} %reshape.322), calls=%async_computation.5 | async-start | bytes 524288 | tf_op jit(solution)/shard_map/all_to_all | solution.py:155
  247.5 5.6 %copy-start.9 = (f32[64,32]{0,1:T(8,128)S(1)}, f32[64,32]{0,1:T(8,128)}, u32[]{:S(2)}) copy-start(f32[64,32]{0,1:T(8,128)} %param.10) | copy-start | bytes 24580
  265.7 1.5 copy-start.11
  265.7 1.5 copy-start.13
  265.7 1.5 copy-start.15
  265.8 4.4 collective-permute-start.1
  270.3 267.7 %copy-start.1 = (f32[32,64]{1,0:T(8,128)S(1)}, f32[32,64]{1,0:T(8,128)}, u32[]{:S(2)}) copy-start(f32[32,64]{1,0:T(8,128)} %param.9) | copy-start | bytes 24580
